TPU v7x, 256 devices: a whole 4x4x8 slice. The times are simulated.
256 devices in a mesh: row: 32 (over y, z), col: 8 (over x, core).
Axes of the slice: x: 4, y: 4, z: 8, core: 2. Of those that a mesh axis runs over, the one named last changes fastest.
Arguments:
- tokens: bfloat16 [1536, 8192], P('row', 'col'), may hold values from -6 to 6
- weight: bfloat16 [8192, 32768], P('col', 'row'), may hold values from -0.109375 to 0.109375
- tile_rows: int32 [32, 8, 32], P('row', 'col'), may hold values from 0 to 63, as said below
- tile_cols: int32 [32, 8, 32], P('row', 'col'), may hold values from 0 to 255, as said below
- tile_count: int32 [32, 8], P('row', 'col'), may hold values from 8 to 32, as said below
- hidden_cotangent: bfloat16 [1536, 32768], P('col', 'row'), may hold values from -6 to 6
Outputs:
- hidden: bfloat16 [1536, 32768], P('col', 'row')
- input_grad: bfloat16 [1536, 8192], P('row', 'col')
- weight_grad: bfloat16 [8192, 32768], P('col', 'row')
Inputs may be any that keep to these rules, and one draw needn't show every extreme that they name: tile_rows[r, c, k] is a row block of the weight (tiles of 128 x 128) among the 8 blocks from c * 8 on, which index c of col holds. tile_cols[r, c, k] is a column block among the 8 blocks from r * 8 on, which index r of row holds; the 32 candidate tiles of one device are distinct. The first tile_count[r, c] candidates of device (r, c) are its nonzero tiles; some device holds 32.
All inputs are finite; a program needn't handle non-finite values.
Results may differ from a plain program's by a relative error of at most 0.0049.
Values may be sent and summed in bfloat16 or wider, within the bound.
No kernel may reach another device: no remote copies, remote signals or barrier semaphores. Data moves between devices by JAX's collectives and lax.ppermute only.
A program may use at most 128 MiB of HBM per device.

v0:
```python
import jax
import jax.numpy as jnp
from jax import lax
from jax.sharding import Mesh
from jax.sharding import PartitionSpec as P

TILE = 128
ROW = ("row_0", "row_1")


def laid_out(pieces, dim):
    pieces = jnp.moveaxis(pieces, 0, dim)
    dims = pieces.shape
    return pieces.reshape(*dims[:dim], dims[dim] * dims[dim + 1], *dims[dim + 2 :])


def all_blocks(shard, axes, turns):
    pieces = shard
    for k in turns:
        pieces = lax.all_gather(pieces, axes[k])
    done = turns[::-1]
    back = [done.index(k) for k in range(len(axes))]
    pieces = pieces.transpose(*back, *range(len(axes), pieces.ndim))
    return pieces.reshape(-1, *shard.shape)


def gathered_by_axis(shard, axes, turns, dim):
    return laid_out(all_blocks(shard, axes, turns), dim)


def own_rows(so_far, axes):
    for axis in axes:
        so_far = lax.psum_scatter(so_far, axis, scatter_dimension=0, tiled=True)
    return so_far


def sparse_apply(inputs, live_tiles, in_index, out_index, out_blocks, flipped):
    count_rows, in_width = inputs.shape
    in_blocks = in_width // TILE
    block_rows = 128
    picker = (in_index[:, None] == jnp.arange(in_blocks)[None, :]).astype(jnp.bfloat16)
    placer = (out_index[:, None] == jnp.arange(out_blocks)[None, :]).astype(jnp.float32)

    def per_block(rows_block):
        shaped_rows = rows_block.reshape(block_rows, in_blocks, TILE)
        pieces = jnp.einsum(
            "bjp,kj->bkp", shaped_rows, picker, preferred_element_type=jnp.float32
        ).astype(jnp.bfloat16)
        if flipped:
            product = jnp.einsum(
                "bkq,kpq->bkp", pieces, live_tiles, preferred_element_type=jnp.float32
            )
        else:
            product = jnp.einsum(
                "bkp,kpq->bkq", pieces, live_tiles, preferred_element_type=jnp.float32
            )
        placed = jnp.einsum("bkq,kc->bcq", product, placer, precision=lax.Precision.HIGHEST)
        return placed.reshape(block_rows, out_blocks * TILE)

    stacked = inputs.reshape(count_rows // block_rows, block_rows, in_width)
    return lax.map(per_block, stacked).reshape(count_rows, out_blocks * TILE)


def tile_grads(full_tokens, full_grads, local_rows, local_cols, is_live, row_blocks, col_blocks):
    count_rows = full_tokens.shape[0]
    block_rows = 128
    steps_count = count_rows // block_rows
    left_side = full_tokens.reshape(steps_count, block_rows, row_blocks, TILE)
    right_side = full_grads.reshape(steps_count, block_rows, col_blocks, TILE)

    def accumulate(running, block_pair):
        token_block, grad_block = block_pair
        product = jnp.einsum(
            "bkp,bkq->kpq",
            token_block[:, local_rows],
            grad_block[:, local_cols],
            preferred_element_type=jnp.float32,
        )
        return (running + product, None)

    start_sums = jnp.zeros((local_rows.shape[0], TILE, TILE), jnp.float32)
    tile_sums, leftover = lax.scan(accumulate, start_sums, (left_side, right_side))
    tile_sums = tile_sums * is_live[:, None, None].astype(jnp.float32)
    slot_ids = local_rows * col_blocks + local_cols
    placed = (
        jnp.zeros((row_blocks * col_blocks, TILE, TILE), jnp.float32).at[slot_ids].add(tile_sums)
    )
    placed = placed.reshape(row_blocks, col_blocks, TILE, TILE).transpose(0, 2, 1, 3)
    return placed.reshape(row_blocks * TILE, col_blocks * TILE).astype(jnp.bfloat16)


def on_device(tokens, weight, tile_rows, tile_cols, tile_count, hidden_cotangent):
    row_index = lax.axis_index(ROW)
    col_index = lax.axis_index("col")
    row_blocks = weight.shape[0] // TILE
    col_blocks = weight.shape[1] // TILE
    capacity = tile_rows.shape[2]
    local_rows = tile_rows.reshape(capacity) - col_index * row_blocks
    local_cols = tile_cols.reshape(capacity) - row_index * col_blocks
    is_live = jnp.arange(capacity) < tile_count.reshape(())
    shaped = weight.reshape(row_blocks, TILE, col_blocks, TILE)
    live_tiles = shaped[local_rows, :, local_cols, :] * is_live[:, None, None].astype(jnp.bfloat16)
    full_tokens = gathered_by_axis(tokens, ROW, (0, 1), 0)
    pre_act = lax.psum_scatter(
        sparse_apply(full_tokens, live_tiles, local_rows, local_cols, col_blocks, False),
        "col",
        scatter_dimension=0,
        tiled=True,
    )
    gate_value = jax.nn.sigmoid(pre_act)
    hidden = (pre_act * gate_value).astype(jnp.bfloat16)
    silu_slope = gate_value * (1.0 + pre_act * (1.0 - gate_value))
    grad_pre = (hidden_cotangent.astype(jnp.float32) * silu_slope).astype(jnp.bfloat16)
    full_grads = lax.all_gather(grad_pre, "col", axis=0, tiled=True)
    input_grad = own_rows(
        sparse_apply(full_grads, live_tiles, local_cols, local_rows, row_blocks, True), ROW
    ).astype(jnp.bfloat16)
    weight_grad = tile_grads(
        full_tokens, full_grads, local_rows, local_cols, is_live, row_blocks, col_blocks
    )
    return (hidden, input_grad, weight_grad)


def solution(mesh):
    split = Mesh(mesh.devices.reshape(4, 8, mesh.shape["col"]), ("row_0", "row_1", "col"))
    placed = (
        P(ROW, "col"),
        P("col", ROW),
        P(ROW, "col", None),
        P(ROW, "col", None),
        P(ROW, "col"),
        P("col", ROW),
    )
    return jax.shard_map(
        on_device,
        mesh=split,
        in_specs=placed,
        out_specs=(P("col", ROW), P(ROW, "col"), P("col", ROW)),
        check_vma=False,
    )
```

profile of v0, /device:TPU:1, one launch (start us, length us, event | category | flops | bytes accessed | tf_op | source)
XLA Modules:
  0.0 455.6 jit_solution(8898258210480005376)
XLA Ops:
  7.2 13.0 %all-gather = bf16[192,1024]{1,0:T(8,128)(2,1)} all-gather(bf16[48,1024]{1,0:T(8,128)(2,1)} %param.12), channel_id=2, replica_groups=mesh['row_0'=4,'row_1'=8,'col'=8] {'row_0'}, dimensions={0}, use_global_device_ids=true | all-gather | bytes 491520 | tf_op jit(solution)/shard_map/all_gather | solution.py:20
  24.8 44.5 %all-gather.7.cloned.1.call-done = bf16[32,48,1024]{2,1,0:T(8,128)(2,1)} async-done(((bf16[4,48,1024]{2,1,0:T(8,128)(2,1)}), bf16[32,48,1024]{2,1,0:T(8,128)(2,1)}) %all-gather.7.cloned.1.call-update) | async-done | bytes 3145744 | tf_op jit(solution)/shard_map/all_gather | solution.py:20
  69.2 4.1 copy.27
  73.3 3.5 broadcast.138.clone
  76.8 66.5 %while.33 = (s32[]{:T(128)}, f32[12,128,1024]{2,1,0:T(8,128)}, bf16[12,128,1024]{2,1,0:T(8,128)(2,1)}, bf16[32,128,128]{2,1,0:T(8,128)(2,1)S(1)}, s32[32]{0:T(128)S(1)}, /*index=5*/s32[32]{0:T(128)S(1)}, s32[]{:T(128)}) while((s32[]{:T(128)}, f32[12,128,1024]{2,1,0:T(8,128)}, bf16[12,128,1024]{2,1,0:T(8,128)(2,1)}, ...), condition=%wide.region_1.2_spmd.clone, body=%wide.region_0.1_spmd.clone.sunk | while | flops 193463296 | bytes 11273041 | solution.py:61
  79.0 2.4 fusion.79
  84.5 2.4 fusion.79
  95.6 2.4 fusion.79
  123.3 2.4 fusion.79
  143.4 43.4 %reduce-scatter.4.cloned.1.call-done = f32[192,1024]{1,0:T(8,128)} async-done(((f32[1536,1024]{1,0:T(8,128)}), f32[192,1024]{1,0:T(8,128)}) %reduce-scatter.4.cloned.1.call-update) | async-done | bytes 786448 | tf_op jit(solution)/shard_map/reduce_scatter | solution.py:104
  186.8 2.4 multiply_convert_fusion
  189.2 31.1 %all-gather.5.cloned.1.call-done = bf16[1536,1024]{1,0:T(8,128)(2,1)} async-done(((bf16[192,1024]{1,0:T(8,128)(2,1)}), bf16[1536,1024]{1,0:T(8,128)(2,1)}) %all-gather.5.cloned.1.call-update) | async-done | bytes 3145744 | tf_op jit(solution)/shard_map/all_gather | solution.py:114
  220.3 3.5 broadcast.138
  223.8 68.4 %while.34 = (s32[]{:T(128)}, f32[12,128,1024]{2,1,0:T(8,128)}, bf16[12,128,1024]{2,1,0:T(8,128)(2,1)}, bf16[32,128,128]{2,1,0:T(8,128)(2,1)S(1)}, s32[32]{0:T(128)S(1)}, /*index=5*/s32[32]{0:T(128)S(1)}, s32[]{:T(128)}) while((s32[]{:T(128)}, f32[12,128,1024]{2,1,0:T(8,128)}, bf16[12,128,1024]{2,1,0:T(8,128)(2,1)}, ...), condition=%wide.region_4.5_spmd.clone, body=%wide.region_3.4_spmd.clone.sunk | while | flops 193463296 | bytes 11273041 | solution.py:61
  294.1 2.6 copy.39
  296.7 2.5 copy.40
  299.1 59.5 %reduce-scatter.6.cloned.1.call-done = f32[384,1024]{1,0:T(8,128)} async-done(((f32[1536,1024]{1,0:T(8,128)}), f32[384,1024]{1,0:T(8,128)}) %reduce-scatter.6.cloned.1.call-update) | async-done | bytes 1572880 | tf_op jit(solution)/shard_map/reduce_scatter | solution.py:33
  358.6 72.4 %while.35 = (s32[]{:T(128)}, f32[32,128,128]{2,1,0:T(8,128)}, bf16[12,128,8,128]{3,2,1,0:T(8,128)(2,1)}, s32[32]{0:T(128)S(1)}, bf16[12,128,8,128]{3,2,1,0:T(8,1...) while((s32[]{:T(128)}, f32[32,128,128]{2,1,0:T(8,128)}, bf16[12,128,8,128]{3,2,1,0:T(8,128)(2,1)}, ...), condition=%wide.region_8.9_spmd.clone, body=%wide.region_7.8_spmd.clone.sunk | while | flops 135268544 | bytes 12592227 | solution.py:82
  365.9 3.4 select_add_fusion.2
  372.1 3.5 select_add_fusion.2
  378.3 3.5 select_add_fusion.2
  384.5 3.5 select_add_fusion.2
  390.6 3.5 select_add_fusion.2
  396.8 3.4 select_add_fusion.2
  403.0 3.4 select_add_fusion.2
  409.1 3.4 select_add_fusion.2
  415.3 3.4 select_add_fusion.2
  421.4 3.4 select_add_fusion.2
  427.6 3.4 select_add_fusion.2
  432.8 2.5 broadcast_in_dim.11
  435.3 6.3 %scatter_fusion = f32[64,128,128]{2,1,0:T(8,128)} fusion(f32[64,128,128]{2,1,0:T(8,128)} %broadcast_in_dim.11, s32[32]{0:T(128)S(1)} %get-tuple-element.217, f32[32,128,128]{2,1,0:T(8,128)S(1)} %broadcast_multiply_fusion), kind=kCustom, calls=%fused_computation.3 | custom fusion | flops 524288 | bytes 6291584 | tf_op jit(solution)/shard_map/scatter-add | solution.py:86
  441.6 2.6 convert_element_type.74
  (295 shorter events, 170.8 us)
Async XLA Ops:
  7.2 62.1 %all-gather.7.cloned.1.call-start = ((), (), s32[]{:S(2)}) async-start(), calls=%async_computation.7 | async-start | bytes 3538944 | tf_op jit(solution)/shard_map/all_gather | solution.py:20
  20.2 166.5 %reduce-scatter.4.cloned.1.call-start = ((), (), s32[]{:S(2)}) async-start(), calls=%async_computation.3 | async-start | bytes 7077888 | tf_op jit(solution)/shard_map/reduce_scatter | solution.py:104
  22.5 1.3 copy-start.3
  22.5 1.3 copy-start.4
  143.3 43.5 %copy-start.2 = (bf16[192,1024]{1,0:T(8,128)(2,1)S(1)}, bf16[192,1024]{1,0:T(8,128)(2,1)}, u32[]{:S(2)}) copy-start(bf16[192,1024]{1,0:T(8,128)(2,1)} %param.17) | copy-start | bytes 1179652
  143.3 77.0 %all-gather.5.cloned.1.call-start = ((), (), s32[]{:S(2)}) async-start(), calls=%async_computation.4 | async-start | bytes 3538944 | tf_op jit(solution)/shard_map/all_gather | solution.py:114
  189.2 169.4 %reduce-scatter.6.cloned.1.call-start = ((), (), s32[]{:S(2)}) async-start(), calls=%async_computation.5 | async-start | bytes 7864320 | tf_op jit(solution)/shard_map/reduce_scatter | solution.py:33
  292.2 1.9 copy-start
  292.2 155.3 %reduce-scatter.8.cloned.1.call-start = ((), (), s32[]{:S(2)}) async-start(), calls=%async_computation.6 | async-start | bytes 1769472 | tf_op jit(solution)/shard_map/reduce_scatter | solution.py:33
  294.1 2.6 copy-start.1
Sparse Core Ops, SparseCore 0:
  20.4 48.8 all-gather.6
  143.4 43.3 reduce-scatter.3
  189.3 30.9 all-gather.4
  292.4 66.2 reduce-scatter.5
  361.0 35.9 reduce-scatter.7
where the time goes:
time: 457 us; the launch traced here: 456 us
  waiting for transfers between devices  179 us (39%)
  matrix products  127 us (28%)
  local copies, waits for them, and re-layouts  105 us (23%)
  other arithmetic  14.9 us (3%)
  between operations  14.6 us (3%)
  blocking collectives  13 us (3%)
    reduce_scatter x2, waiting for transfers between devices, own_rows(): so_far = lax.psum_scatter(so_far, axis, scatter_dimension=0, tiled=True)  59.5 us
    dot_general x24, matrix products, per_block(): jnp.einsum('bkq,kc->bcq', product, placer, precision=lax.Precision.HIGHEST)  56.6 us
    all_gather x1, waiting for transfers between devices, all_blocks(): pieces = lax.all_gather(pieces, axes[k])  44.5 us
    reduce_scatter x1, waiting for transfers between devices, on_device(): lax.psum_scatter(sparse_apply(full_tokens, live_tiles, local_rows, local_...  43.4 us
    dot_general x12, matrix products, accumulate(): jnp.einsum('bkp,bkq->kpq', token_block[:, local_rows], grad_block[:, loca...  39.8 us
    all_gather x1, waiting for transfers between devices, on_device(): full_grads = lax.all_gather(grad_pre, 'col', axis=0, tiled=True)  31.1 us
    while x48, local copies, waits for them, and re-layouts  24.3 us
    dynamic_update_slice x24, local copies, waits for them, and re-layouts, sparse_apply(): return lax.map(per_block, stacked).reshape(count_rows, out_blocks * TILE)  20.5 us
  transfers between devices with their start and end apart: 5, of which 4 were waited for; matrix products, arithmetic and copies ran while one was open for 21% of the time, Pallas kernels for 0%

commit v1 on v0

--- a/solution.py
+++ b/solution.py
@@ -111,7 +111,9 @@
     hidden = (pre_act * gate_value).astype(jnp.bfloat16)
     silu_slope = gate_value * (1.0 + pre_act * (1.0 - gate_value))
     grad_pre = (hidden_cotangent.astype(jnp.float32) * silu_slope).astype(jnp.bfloat16)
-    full_grads = lax.all_gather(grad_pre, "col", axis=0, tiled=True)
+    full_grads = jnp.concatenate(
+        lax.all_to_all(jnp.stack([grad_pre] * lax.axis_size("col")), "col", 0, 0), axis=0
+    )
     input_grad = own_rows(
         sparse_apply(full_grads, live_tiles, local_cols, local_rows, row_blocks, True), ROW
     ).astype(jnp.bfloat16)

time: 457 us -> 471 us (1.031)
  starting transfers between devices: 0.39 us -> 5.84 us
  local copies, waits for them, and re-layouts: 105 us -> 110 us
    all_to_all x0 -> x1, waiting for transfers between devices: none -> 37.7 us  [on_device(): lax.all_to_all(jnp.stack([grad_pre] * lax.axis_size('col')), 'col', 0, 0)]
    all_gather x1 -> x0, waiting for transfers between devices: 31.1 us -> none  [on_device(): full_grads = lax.all_gather(grad_pre, 'col', axis=0, tiled=True)]
    all_to_all x0 -> x1, starting transfers between devices: none -> 5.53 us  [on_device(): lax.all_to_all(jnp.stack([grad_pre] * lax.axis_size('col')), 'col', 0, 0)]
    unnamed x14 -> x10, local copies, waits for them, and re-layouts: 10.8 us -> 13 us
  transfers between devices with their start and end apart: 5 -> 5, of which waited for: 4 -> 4; matrix products, arithmetic and copies ran while one was open for 21% -> 22% of each run, Pallas kernels for 0% -> 0%
where the time goes in v1:
time: 471 us; the launch traced here: 469 us
  waiting for transfers between devices  181 us (38%)
  matrix products  127 us (27%)
  local copies, waits for them, and re-layouts  110 us (23%)
  other arithmetic  16 us (3%)
  between operations  14.5 us (3%)
  blocking collectives  13 us (3%)
  starting transfers between devices  5.84 us (1%)
    reduce_scatter x2, waiting for transfers between devices, own_rows(): so_far = lax.psum_scatter(so_far, axis, scatter_dimension=0, tiled=True)  57.4 us
    dot_general x24, matrix products, per_block(): jnp.einsum('bkq,kc->bcq', product, placer, precision=lax.Precision.HIGHEST)  56.6 us
    reduce_scatter x1, waiting for transfers between devices, on_device(): lax.psum_scatter(sparse_apply(full_tokens, live_tiles, local_rows, local_...  43.5 us
    all_gather x1, waiting for transfers between devices, all_blocks(): pieces = lax.all_gather(pieces, axes[k])  42.4 us
    dot_general x12, matrix products, accumulate(): jnp.einsum('bkp,bkq->kpq', token_block[:, local_rows], grad_block[:, loca...  39.8 us
    all_to_all x1, waiting for transfers between devices, on_device(): lax.all_to_all(jnp.stack([grad_pre] * lax.axis_size('col')), 'col', 0, 0)  37.7 us
    while x48, local copies, waits for them, and re-layouts  24.3 us
    dynamic_update_slice x24, local copies, waits for them, and re-layouts, sparse_apply(): return lax.map(per_block, stacked).reshape(count_rows, out_blocks * TILE)  20.3 us
  transfers between devices with their start and end apart: 5, of which 4 were waited for; matrix products, arithmetic and copies ran while one was open for 22% of the time, Pallas kernels for 0%

profile of v1, /device:TPU:1, one launch (start us, length us, event | category | flops | bytes accessed | tf_op | source)
XLA Modules:
  0.0 469.3 jit_solution(12096203566393115666)
XLA Ops:
  7.2 13.0 %all-gather = bf16[192,1024]{1,0:T(8,128)(2,1)} all-gather(bf16[48,1024]{1,0:T(8,128)(2,1)} %param.12), channel_id=2, replica_groups=mesh['row_0'=4,'row_1'=8,'col'=8] {'row_0'}, dimensions={0}, use_global_device_ids=true | all-gather | bytes 491520 | tf_op jit(solution)/shard_map/all_gather | solution.py:20
  26.8 42.4 %all-gather.4.cloned.1.call-done = bf16[32,48,1024]{2,1,0:T(8,128)(2,1)} async-done(((bf16[4,48,1024]{2,1,0:T(8,128)(2,1)}), bf16[32,48,1024]{2,1,0:T(8,128)(2,1)}) %all-gather.4.cloned.1.call-update) | async-done | bytes 3145744 | tf_op jit(solution)/shard_map/all_gather | solution.py:20
  69.2 4.1 copy.26
  73.3 3.4 broadcast.140.clone
  76.8 66.4 %while.33 = (s32[]{:T(128)}, f32[12,128,1024]{2,1,0:T(8,128)}, bf16[12,128,1024]{2,1,0:T(8,128)(2,1)}, bf16[32,128,128]{2,1,0:T(8,128)(2,1)S(1)}, s32[32]{0:T(128)S(1)}, /*index=5*/s32[32]{0:T(128)S(1)}, s32[]{:T(128)}) while((s32[]{:T(128)}, f32[12,128,1024]{2,1,0:T(8,128)}, bf16[12,128,1024]{2,1,0:T(8,128)(2,1)}, ...), condition=%wide.region_1.2_spmd.clone, body=%wide.region_0.1_spmd.clone.sunk | while | flops 193463296 | bytes 11273041 | solution.py:61
  95.6 2.4 fusion.79
  112.2 2.4 fusion.79
  117.8 2.4 fusion.79
  128.8 2.4 fusion.79
  143.2 43.5 %reduce-scatter.4.cloned.1.call-done = f32[192,1024]{1,0:T(8,128)} async-done(((f32[1536,1024]{1,0:T(8,128)}), f32[192,1024]{1,0:T(8,128)}) %reduce-scatter.4.cloned.1.call-update) | async-done | bytes 786448 | tf_op jit(solution)/shard_map/reduce_scatter | solution.py:104
  191.0 5.5 %all-to-all-start = ((bf16[8,192,1024]{2,1,0:T(8,128)(2,1)}), bf16[8,192,1024]{2,1,0:T(8,128)(2,1)}, u32[]{:S(2)}, u32[]{:S(2)}) async-start(bf16[8,192,1024]{2,1,0:T(8,128)(2,1)} %stack.2), calls=%async_computation.1 | async-start | bytes 6291456 | tf_op jit(solution)/shard_map/all_to_all | solution.py:115
  196.5 37.7 %all-to-all-done = bf16[8,192,1024]{2,1,0:T(8,128)(2,1)} async-done(((bf16[8,192,1024]{2,1,0:T(8,128)(2,1)}), bf16[8,192,1024]{2,1,0:T(8,128)(2,1)}, u32[]{:S(2)}, u32[]{:S(2)}) %all-to-all-start) | async-done | bytes 3145760 | tf_op jit(solution)/shard_map/all_to_all | solution.py:115
  234.2 3.4 broadcast.140
  237.6 68.3 %while.34 = (s32[]{:T(128)}, f32[12,128,1024]{2,1,0:T(8,128)}, bf16[12,128,1024]{2,1,0:T(8,128)(2,1)}, bf16[32,128,128]{2,1,0:T(8,128)(2,1)S(1)}, s32[32]{0:T(128)S(1)}, /*index=5*/s32[32]{0:T(128)S(1)}, s32[]{:T(128)}) while((s32[]{:T(128)}, f32[12,128,1024]{2,1,0:T(8,128)}, bf16[12,128,1024]{2,1,0:T(8,128)(2,1)}, ...), condition=%wide.region_4.5_spmd.clone, body=%wide.region_3.4_spmd.clone.sunk | while | flops 193463296 | bytes 11273041 | solution.py:61
  306.2 4.4 copy.38
  310.6 4.4 copy.39
  315.0 57.4 %reduce-scatter.6.cloned.1.call-done = f32[384,1024]{1,0:T(8,128)} async-done(((f32[1536,1024]{1,0:T(8,128)}), f32[384,1024]{1,0:T(8,128)}) %reduce-scatter.6.cloned.1.call-update) | async-done | bytes 1572880 | tf_op jit(solution)/shard_map/reduce_scatter | solution.py:33
  372.4 72.4 %while.35 = (s32[]{:T(128)}, f32[32,128,128]{2,1,0:T(8,128)}, bf16[12,128,8,128]{3,2,1,0:T(8,128)(2,1)}, s32[32]{0:T(128)S(1)}, bf16[12,128,8,128]{3,2,1,0:T(8,1...) while((s32[]{:T(128)}, f32[32,128,128]{2,1,0:T(8,128)}, bf16[12,128,8,128]{3,2,1,0:T(8,128)(2,1)}, ...), condition=%wide.region_8.9_spmd.clone, body=%wide.region_7.8_spmd.clone.sunk | while | flops 135268544 | bytes 12592227 | solution.py:82
  379.7 3.4 select_add_fusion.2
  385.9 3.5 select_add_fusion.2
  392.1 3.5 select_add_fusion.2
  398.2 3.5 select_add_fusion.2
  404.4 3.5 select_add_fusion.2
  410.6 3.5 select_add_fusion.2
  416.8 3.4 select_add_fusion.2
  422.9 3.4 select_add_fusion.2
  429.1 3.4 select_add_fusion.2
  435.2 3.4 select_add_fusion.2
  441.4 3.4 select_add_fusion.2
  446.6 2.5 broadcast_in_dim.11
  449.1 6.2 %scatter_fusion = f32[64,128,128]{2,1,0:T(8,128)} fusion(f32[64,128,128]{2,1,0:T(8,128)} %broadcast_in_dim.11, s32[32]{0:T(128)S(1)} %get-tuple-element.211, f32[32,128,128]{2,1,0:T(8,128)S(1)} %broadcast_multiply_fusion), kind=kCustom, calls=%fused_computation.3 | custom fusion | flops 524288 | bytes 6291584 | tf_op jit(solution)/shard_map/scatter-add | solution.py:86
  455.3 2.6 convert_element_type.74
  (291 shorter events, 175.3 us)
Async XLA Ops:
  7.2 62.1 %all-gather.4.cloned.1.call-start = ((), (), s32[]{:S(2)}) async-start(), calls=%async_computation.7 | async-start | bytes 3538944 | tf_op jit(solution)/shard_map/all_gather | solution.py:20
  20.2 166.5 %reduce-scatter.4.cloned.1.call-start = ((), (), s32[]{:S(2)}) async-start(), calls=%async_computation.4 | async-start | bytes 7077888 | tf_op jit(solution)/shard_map/reduce_scatter | solution.py:104
  22.5 1.3 copy-start.1
  22.5 1.3 copy-start.2
  143.2 43.5 %copy-start = (bf16[192,1024]{1,0:T(8,128)(2,1)S(1)}, bf16[192,1024]{1,0:T(8,128)(2,1)}, u32[]{:S(2)}) copy-start(bf16[192,1024]{1,0:T(8,128)(2,1)} %param.17) | copy-start | bytes 1179652
  191.0 43.2 %all-to-all-start = ((bf16[8,192,1024]{2,1,0:T(8,128)(2,1)}), bf16[8,192,1024]{2,1,0:T(8,128)(2,1)}, u32[]{:S(2)}, u32[]{:S(2)}) async-start(bf16[8,192,1024]{2,1,0:T(8,128)(2,1)} %stack.2), calls=%async_computation.1 | async-start | bytes 6291456 | tf_op jit(solution)/shard_map/all_to_all | solution.py:115
  196.5 175.9 %reduce-scatter.6.cloned.1.call-start = ((), (), s32[]{:S(2)}) async-start(), calls=%async_computation.5 | async-start | bytes 7864320 | tf_op jit(solution)/shard_map/reduce_scatter | solution.py:33
  306.0 155.2 %reduce-scatter.8.cloned.1.call-start = ((), (), s32[]{:S(2)}) async-start(), calls=%async_computation.6 | async-start | bytes 1769472 | tf_op jit(solution)/shard_map/reduce_scatter | solution.py:33
Sparse Core Ops, SparseCore 0:
  20.4 48.8 all-gather.3
  143.3 43.3 reduce-scatter.3
  306.1 66.2 reduce-scatter.5
  374.8 36.1 reduce-scatter.7
